TPU v7x, 32 devices: a whole 2x2x4 slice. The times are simulated.
32 devices in a mesh: island: 4 (over z), fsdp: 2 (over x), tensor: 4 (over y, core).
Axes of the slice: x: 2, y: 2, z: 4, core: 2. Of those that a mesh axis runs over, the one named last changes fastest.
Arguments:
- hidden: bfloat16 [4, 256, 14336], P('island', 'fsdp', 'tensor'), may hold values from -6 to 6
- target: bfloat16 [4, 256, 4096], P('island', 'tensor', 'fsdp'), may hold values from -6 to 6
- valid: int32 [4, 256], P('island', 'fsdp'), may hold values from 0 to 1, as said below
- island_tokens: int32 [4], replicated, may hold values from 4096 to 16384
- inner_weight: bfloat16 [4, 14336, 4096], P('island', 'tensor', 'fsdp'), may hold values from -6 to 6
- adam_first: bfloat16 [4, 14336, 4096], P('island', 'tensor', 'fsdp'), may hold values from -0.0014648438 to 0.0014648438
- adam_second: bfloat16 [4, 14336, 4096], P('island', 'tensor', 'fsdp'), may hold values from 6.798655e-08 to 1.0877848e-06
- anchor: bfloat16 [14336, 4096], P('tensor', 'fsdp'), may hold values from -6 to 6
- outer_momentum: bfloat16 [14336, 4096], P('tensor', 'fsdp'), may hold values from -6 to 6
Outputs:
- new_weight: bfloat16 [14336, 4096], P('tensor', 'fsdp')
- new_momentum: bfloat16 [14336, 4096], P('tensor', 'fsdp')
Inputs may be any that keep to these rules, and one draw needn't show every extreme that they name: The first token of each block of 128 tokens is valid.
All inputs are finite; a program needn't handle non-finite values.
Results may differ from a plain program's by a relative error of at most 0.003.
Values may be sent and summed in bfloat16 or wider, within the bound.
No kernel may reach another device: no remote copies, remote signals or barrier semaphores. Data moves between devices by JAX's collectives and lax.ppermute only.
A program may use at most 320 MiB of HBM per device.

v0:
```python
import jax
import jax.numpy as jnp
from jax import lax
from jax.sharding import PartitionSpec as P

FFW = 14336
beta_first = 0.9
beta_second = 0.95
epsilon = 1e-08
inner_rate = 0.5
decay_rate = 0.1
outer_rate = 0.7
nesterov_mu = 0.9


def nesterov(anchor_part, moment_part, average_step):
    momentum = nesterov_mu * moment_part.astype(jnp.float32) + average_step
    updated = anchor_part.astype(jnp.float32) - outer_rate * (average_step + nesterov_mu * momentum)
    return (updated.astype(jnp.bfloat16), momentum.astype(jnp.bfloat16))


def on_device(
    hidden,
    target,
    valid,
    island_tokens,
    inner_weight,
    adam_first,
    adam_second,
    anchor,
    outer_momentum,
):
    factor = FFW ** (-0.5)
    keep_mask = valid[0].astype(jnp.bfloat16)
    masked = hidden[0] * keep_mask[:, None]
    tallies = lax.psum(jnp.sum(valid[0].astype(jnp.float32)), "fsdp")
    gathered = lax.all_gather(masked, "fsdp", axis=0, tiled=True)
    partial_out = factor * jnp.dot(gathered, inner_weight[0], preferred_element_type=jnp.float32)
    full_target = lax.all_gather(target[0], "tensor", axis=0, tiled=True)
    summed = lax.psum(partial_out.astype(jnp.bfloat16), "tensor").astype(jnp.float32)
    cotangent = ((summed - full_target.astype(jnp.float32)) / tallies).astype(jnp.bfloat16)
    gradient = factor * lax.dot_general(
        gathered, cotangent, (((0,), (0,)), ((), ())), preferred_element_type=jnp.float32
    )
    weights = inner_weight[0].astype(jnp.float32)
    first = beta_first * adam_first[0].astype(jnp.float32) + (1.0 - beta_first) * gradient
    second = (
        beta_second * adam_second[0].astype(jnp.float32) + (1.0 - beta_second) * gradient * gradient
    )
    inner_new = weights - inner_rate * (first / (jnp.sqrt(second) + epsilon) + decay_rate * weights)
    totals = island_tokens.astype(jnp.float32)
    portion = totals[lax.axis_index("island")] / jnp.sum(totals)
    weighted = portion * (anchor.astype(jnp.float32) - inner_new)
    average_step = lax.psum(weighted, "island")
    return nesterov(anchor, outer_momentum, average_step)


def solution(mesh):
    return jax.shard_map(
        on_device,
        mesh=mesh,
        in_specs=(
            P("island", "fsdp", "tensor"),
            P("island", "tensor", "fsdp"),
            P("island", "fsdp"),
            P(),
            P("island", "tensor", "fsdp"),
            P("island", "tensor", "fsdp"),
            P("island", "tensor", "fsdp"),
            P("tensor", "fsdp"),
            P("tensor", "fsdp"),
        ),
        out_specs=(P("tensor", "fsdp"), P("tensor", "fsdp")),
        check_vma=False,
    )
```

profile of v0, /device:TPU:0, one launch (start us, length us, event | category | flops | bytes accessed | tf_op | source)
XLA Modules:
  0.0 1147.3 jit_solution(17382033286298603500)
XLA Ops:
  7.2 0.0 copy-start.1
  7.2 0.0 copy-start.2
  7.2 0.0 all-gather.4.cloned.1.call-start
  7.2 0.7 convert_bitcast_fusion
  7.9 2.2 bitcast_multiply_fusion
  10.1 0.0 all-gather.4.cloned.1.call-update
  10.2 0.0 all-gather.6.cloned.1.call-start
  10.2 0.7 all-gather.6.cloned.1.call-update
  10.9 0.0 all-reduce.3.cloned.1.call-start
  11.0 32.2 %all-gather.4.cloned.1.call-done = bf16[256,3584]{1,0:T(8,128)(2,1)} async-done(((bf16[128,3584]{1,0:T(8,128)(2,1)}), bf16[256,3584]{1,0:T(8,128)(2,1)}) %all-gather.4.cloned.1.call-update) | async-done | bytes 1835024 | tf_op jit(solution)/shard_map/all_gather | solution.py:37
  43.2 0.0 copy-start
  43.2 10.8 fusion.13
  54.0 0.0 all-reduce.3.cloned.1.call-update
  54.0 0.0 all-reduce.5.cloned.1.call-start
  54.0 0.0 copy-done.1
  54.0 0.6 convert_reduce_fusion
  54.7 5.8 psum.22
  60.5 0.0 copy-done.2
  60.5 0.6 dynamic_slice.3
  61.1 0.7 convert_reduce_fusion.1
  63.1 0.0 all-gather.6.cloned.1.call-done
  63.1 37.4 %all-reduce.3.cloned.1.call-done = bf16[256,2048]{1,0:T(8,128)(2,1)} async-done(((bf16[256,2048]{1,0:T(8,128)(2,1)}), bf16[256,2048]{1,0:T(8,128)(2,1)}) %all-reduce.3.cloned.1.call-update) | async-done | bytes 1048592 | tf_op jit(solution)/shard_map/psum | solution.py:40
  100.6 0.0 copy-done
  100.6 40.1 %fusion = f32[3584,2048]{1,0:T(8,128)} fusion(bf16[3584,2048]{1,0:T(8,128)(2,1)} %param.16, bf16[1,3584,2048]{2,1,0:T(8,128)(2,1)} %param.15, bf16[1,3584,2048]{2,1,0:T(8,128)(2,1)} %param.14, bf16[1,3584,2048]{2,1,0:T(8,128)(2,1)} %param.13, f32[]{:T(128)S(6)} %div.12, bf16[256,3584]{1,0:T(8,128)(2,1)S(1)} %copy-done, ...), kind=kOutput, calls=%fused_computation.4 | convolution fusion | flops 3907518464 | bytes 92012552 | tf_op jit(solution)/shard_map/dot_general | solution.py:42
  140.6 0.0 all-reduce.5.cloned.1.call-update
  140.7 968.3 %all-reduce.5.cloned.1.call-done = f32[3584,2048]{1,0:T(8,128)} async-done(((f32[3584,2048]{1,0:T(8,128)}), f32[3584,2048]{1,0:T(8,128)}) %all-reduce.5.cloned.1.call-update) | async-done | bytes 29360144 | tf_op jit(solution)/shard_map/psum | solution.py:54
  1108.9 31.9 %fusion.7 = (bf16[3584,2048]{1,0:T(8,128)(2,1)}, bf16[3584,2048]{1,0:T(8,128)(2,1)}) fusion(f32[3584,2048]{1,0:T(8,128)} %all-reduce.5.cloned.1.call-done, bf16[3584,2048]{1,0:T(8,128)(2,1)} %param.17, bf16[3584,2048]{1,0:T(8,128)(2,1)} %param.16), kind=kLoop, calls=%fused_computation.14 | loop fusion | flops 73400320 | bytes 88080384 | tf_op jit(solution)/shard_map/convert_element_type | solution.py:19
  (1 shorter events, 0.0 us)
Async XLA Ops:
  7.2 46.9 %copy-start.1 = (s32[1,128]{1,0:T(1,128)S(1)}, s32[1,128]{1,0:T(1,128)}, u32[]{:S(2)}) copy-start(s32[1,128]{1,0:T(1,128)} %param.11) | copy-start | bytes 1540
  7.2 53.3 %copy-start.2 = (s32[4]{0:T(128)S(1)}, s32[4]{0:T(128)}, u32[]{:S(2)}) copy-start(s32[4]{0:T(128)} %param.12) | copy-start | bytes 52
  7.2 36.0 %all-gather.4.cloned.1.call-start = ((), (), s32[]{:S(2)}) async-start(), calls=%async_computation | async-start | bytes 2752512 | tf_op jit(solution)/shard_map/all_gather | solution.py:37
  10.2 53.0 %all-gather.6.cloned.1.call-start = ((), (), s32[]{:S(2)}) async-start(), calls=%async_computation.3 | async-start | bytes 1310720 | tf_op jit(solution)/shard_map/all_gather | solution.py:39
  10.9 89.6 %all-reduce.3.cloned.1.call-start = ((), (), s32[]{:S(2)}) async-start(), calls=%async_computation.1 | async-start | bytes 2097152 | tf_op jit(solution)/shard_map/psum | solution.py:40
  43.2 57.4 %copy-start = (bf16[256,3584]{1,0:T(8,128)(2,1)S(1)}, bf16[256,3584]{1,0:T(8,128)(2,1)}, u32[]{:S(2)}) copy-start(bf16[256,3584]{1,0:T(8,128)(2,1)} %all-gather.4.cloned.1.call-done) | copy-start | bytes 5505028
  54.0 1054.9 %all-reduce.5.cloned.1.call-start = ((), (), s32[]{:S(2)}) async-start(), calls=%async_computation.2 | async-start | bytes 58720256 | tf_op jit(solution)/shard_map/psum | solution.py:54
Sparse Core Ops, SparseCore 0:
  10.3 32.8 all-gather.3
  44.7 16.7 all-gather.5
  64.4 36.0 all-reduce.2
  140.8 968.0 all-reduce.4
where the time goes:
time: 1150 us
  waiting for transfers between devices  1040 us (90%)
  matrix products  50.9 us (4%)
  other arithmetic  36 us (3%)
  between operations  15.2 us (1%)
    psum x1, waiting for transfers between devices, on_device(): average_step = lax.psum(weighted, 'island')  968 us
    dot_general x1, matrix products, on_device(): lax.dot_general(gathered, cotangent, (((0,), (0,)), ((), ())), preferred_...  40.1 us
    psum x1, waiting for transfers between devices, on_device(): lax.psum(partial_out.astype(jnp.bfloat16), 'tensor').astype(jnp.float32)  37.4 us
    all_gather x1, waiting for transfers between devices, on_device(): gathered = lax.all_gather(masked, 'fsdp', axis=0, tiled=True)  32.2 us
    convert_element_type x1, other arithmetic, nesterov(): return (updated.astype(jnp.bfloat16), momentum.astype(jnp.bfloat16))  31.9 us
  transfers between devices with their start and end apart: 4, of which 3 were waited for; matrix products, arithmetic and copies ran while one was open for 1% of the time, Pallas kernels for 0%

commit v1 on v0

--- a/solution.py
+++ b/solution.py
@@ -1,7 +1,9 @@
+import functools
 import jax
 import jax.numpy as jnp
 from jax import lax
 from jax.sharding import PartitionSpec as P
+from jax.lax import all_gather
 
 FFW = 14336
 beta_first = 0.9
@@ -11,6 +13,14 @@
 decay_rate = 0.1
 outer_rate = 0.7
 nesterov_mu = 0.9
+
+
+def define_ratios_here(x_local, net_axis):
+    big = all_gather(x_local, axis_name=net_axis)
+    return jnp.sum(big, axis=0)
+
+
+cut_the_yards = functools.partial(define_ratios_here, net_axis="island")
 
 
 def nesterov(anchor_part, moment_part, average_step):
@@ -51,7 +61,7 @@
     totals = island_tokens.astype(jnp.float32)
     portion = totals[lax.axis_index("island")] / jnp.sum(totals)
     weighted = portion * (anchor.astype(jnp.float32) - inner_new)
-    average_step = lax.psum(weighted, "island")
+    average_step = cut_the_yards(weighted)
     return nesterov(anchor, outer_momentum, average_step)
 
 

time: 1150 us -> 2160 us (1.88)
  waiting for transfers between devices: 1040 us -> 2010 us
  other arithmetic: 36 us -> 83.2 us
    all_gather x0 -> x1, waiting for transfers between devices: none -> 1940 us  [define_ratios_here(): big = all_gather(x_local, axis_name=net_axis)]
    psum x1 -> x0, waiting for transfers between devices: 968 us -> none  [on_device(): average_step = lax.psum(weighted, 'island')]
    reduce_sum x0 -> x1, other arithmetic: none -> 47.2 us  [define_ratios_here(): return jnp.sum(big, axis=0)]
where the time goes in v1:
time: 2160 us
  waiting for transfers between devices  2010 us (93%)
  other arithmetic  83.2 us (4%)
  matrix products  51.1 us (2%)
    all_gather x1, waiting for transfers between devices, define_ratios_here(): big = all_gather(x_local, axis_name=net_axis)  1940 us
    reduce_sum x1, other arithmetic, define_ratios_here(): return jnp.sum(big, axis=0)  47.2 us
  transfers between devices with their start and end apart: 4, of which 3 were waited for; matrix products, arithmetic and copies ran while one was open for 1% of the time, Pallas kernels for 0%

profile of v1, /device:TPU:0, one launch (start us, length us, event | category | flops | bytes accessed | tf_op | source)
XLA Modules:
  0.0 2161.5 jit_solution(16520393599806580842)
XLA Ops:
  7.2 0.0 copy-start.1
  7.2 0.0 copy-start.2
  7.2 0.0 all-gather.6.cloned.1.call-start
  7.2 0.7 convert_bitcast_fusion
  7.9 2.2 bitcast_multiply_fusion
  10.1 0.0 all-gather.6.cloned.1.call-update
  10.2 0.0 all-gather.8.cloned.1.call-start
  10.2 0.7 all-gather.8.cloned.1.call-update
  10.9 0.0 all-reduce.2.cloned.1.call-start
  11.0 32.2 %all-gather.6.cloned.1.call-done = bf16[256,3584]{1,0:T(8,128)(2,1)} async-done(((bf16[128,3584]{1,0:T(8,128)(2,1)}), bf16[256,3584]{1,0:T(8,128)(2,1)}) %all-gather.6.cloned.1.call-update) | async-done | bytes 1835024 | tf_op jit(solution)/shard_map/all_gather | solution.py:47
  43.2 0.0 copy-start
  43.2 10.8 fusion.13
  54.0 0.0 all-reduce.2.cloned.1.call-update
  54.0 0.0 all-gather.10.cloned.1.call-start
  54.0 0.0 copy-done.1
  54.0 0.6 convert_reduce_fusion
  54.6 5.8 psum.15
  60.4 0.0 copy-done.2
  60.4 0.6 dynamic_slice.3
  61.0 0.6 convert_reduce_fusion.1
  62.9 0.0 all-gather.8.cloned.1.call-done
  63.0 37.7 %all-reduce.2.cloned.1.call-done = bf16[256,2048]{1,0:T(8,128)(2,1)} async-done(((bf16[256,2048]{1,0:T(8,128)(2,1)}), bf16[256,2048]{1,0:T(8,128)(2,1)}) %all-reduce.2.cloned.1.call-update) | async-done | bytes 1048592 | tf_op jit(solution)/shard_map/psum | solution.py:50
  100.6 0.0 copy-done
  100.6 40.3 %fusion = f32[3584,2048]{1,0:T(8,128)} fusion(bf16[3584,2048]{1,0:T(8,128)(2,1)} %param.16, bf16[1,3584,2048]{2,1,0:T(8,128)(2,1)} %param.15, bf16[1,3584,2048]{2,1,0:T(8,128)(2,1)} %param.14, bf16[1,3584,2048]{2,1,0:T(8,128)(2,1)} %param.13, f32[]{:T(128)S(6)} %div.12, bf16[256,3584]{1,0:T(8,128)(2,1)S(1)} %copy-done, ...), kind=kOutput, calls=%fused_computation.4 | convolution fusion | flops 3907518464 | bytes 92012552 | tf_op jit(solution)/shard_map/dot_general | solution.py:52
  140.9 0.0 all-gather.10.cloned.1.call-update
  140.9 1935.0 %all-gather.10.cloned.1.call-done = f32[14336,2048]{1,0:T(8,128)} async-done(((f32[3584,2048]{1,0:T(8,128)}), f32[14336,2048]{1,0:T(8,128)}) %all-gather.10.cloned.1.call-update) | async-done | bytes 117440528 | tf_op jit(solution)/shard_map/all_gather | solution.py:19
  2075.9 47.2 %reduce_sum.29 = f32[3584,2048]{1,0:T(8,128)} reduce(f32[4,3584,2048]{2,1,0:T(8,128)} %bitcast.7, f32[]{:T(128)} %constant.6.clone.1), dimensions={0}, to_apply=%region_4.0 | reduce | flops 22020096 | bytes 146800640 | tf_op jit(solution)/shard_map/reduce_sum | solution.py:20
  2123.1 31.9 %fusion.7 = (bf16[3584,2048]{1,0:T(8,128)(2,1)}, bf16[3584,2048]{1,0:T(8,128)(2,1)}) fusion(f32[3584,2048]{1,0:T(8,128)} %reduce_sum.29, bf16[3584,2048]{1,0:T(8,128)(2,1)} %param.17, bf16[3584,2048]{1,0:T(8,128)(2,1)} %param.16), kind=kLoop, calls=%fused_computation.14 | loop fusion | flops 73400320 | bytes 88080384 | tf_op jit(solution)/shard_map/convert_element_type | solution.py:29
  (1 shorter events, 0.0 us)
Async XLA Ops:
  7.2 46.9 %copy-start.1 = (s32[1,128]{1,0:T(1,128)S(1)}, s32[1,128]{1,0:T(1,128)}, u32[]{:S(2)}) copy-start(s32[1,128]{1,0:T(1,128)} %param.11) | copy-start | bytes 1540
  7.2 53.2 %copy-start.2 = (s32[4]{0:T(128)S(1)}, s32[4]{0:T(128)}, u32[]{:S(2)}) copy-start(s32[4]{0:T(128)} %param.12) | copy-start | bytes 52
  7.2 36.0 %all-gather.6.cloned.1.call-start = ((), (), s32[]{:S(2)}) async-start(), calls=%async_computation | async-start | bytes 2752512 | tf_op jit(solution)/shard_map/all_gather | solution.py:47
  10.2 52.8 %all-gather.8.cloned.1.call-start = ((), (), s32[]{:S(2)}) async-start(), calls=%async_computation.2 | async-start | bytes 1310720 | tf_op jit(solution)/shard_map/all_gather | solution.py:49
  10.9 89.7 %all-reduce.2.cloned.1.call-start = ((), (), s32[]{:S(2)}) async-start(), calls=%async_computation.1 | async-start | bytes 2097152 | tf_op jit(solution)/shard_map/psum | solution.py:50
  43.2 57.4 %copy-start = (bf16[256,3584]{1,0:T(8,128)(2,1)S(1)}, bf16[256,3584]{1,0:T(8,128)(2,1)}, u32[]{:S(2)}) copy-start(bf16[256,3584]{1,0:T(8,128)(2,1)} %all-gather.6.cloned.1.call-done) | copy-start | bytes 5505028
  54.0 2021.9 %all-gather.10.cloned.1.call-start = ((), (), s32[]{:S(2)}) async-start(), calls=%async_computation.3 | async-start | bytes 146800640 | tf_op jit(solution)/shard_map/all_gather | solution.py:19
Sparse Core Ops, SparseCore 0:
  10.3 32.8 all-gather.5
  44.7 16.7 all-gather.7
  64.4 36.1 all-reduce.1
  141.0 1934.8 all-gather.9
